TPU v7x, 32 devices: a whole 2x2x4 slice. The times are simulated.
32 devices in a mesh: store: 8 (over y, x, core), vocab: 4 (over z).
Axes of the slice: x: 2, y: 2, z: 4, core: 2. Of those that a mesh axis runs over, the one named last changes fastest.
Arguments:
- hidden: bfloat16 [512, 4096], P('store')
- lm_head: bfloat16 [4096, 65536], P(None, ('store', 'vocab'))
- store_keys: bfloat16 [8192, 4096], P(('store', 'vocab'))
- values: int32 [8192], P(('store', 'vocab')), may hold values from 0 to 65535, as said below
- licences: int32 [8192], P(('store', 'vocab')), may hold values from 0 to 29, as said below
- allowed: int32 [512], replicated, may hold values from 1 to 1073741823, as said below
Outputs:
- log_probs: float32 [512, 65536], P(None, ('store', 'vocab'))
Inputs may be any that keep to these rules, and one draw needn't show every extreme that they name: `values`: entry i holds a token t with t // 2048 = (i // 1024) * 4 + (i // 64) % 4: the entries of a device name tokens of the 8192 columns of its index along store, and its k-th run of 64 entries names tokens of the k-th 2048 columns of those. `licences`: some entry has licence 0. `allowed`: bit l of a position's word says whether licence l may be used; bit 0 is always set.
All inputs are finite; a program needn't handle non-finite values.
Results may differ from a plain program's by a relative error of at most 0.0003.
Values may be sent and summed in bfloat16 or wider, within the bound.
A program may use at most 128 MiB of HBM per device.

v0:
```python
import math
import jax
import jax.numpy as jnp
from jax import lax
from jax.sharding import PartitionSpec as P

NEG_FILL = -1e30


def mixture(lm_log, knn_mass, knn_total):
    share = knn_mass / knn_total[:, None]
    present = share > 0.0
    knn_log = jnp.where(present, jnp.log(jnp.where(present, share, 1.0)), -jnp.inf)
    return jnp.logaddexp(math.log(0.75) + lm_log, math.log(0.25) + knn_log)


def bin_tokens(weights, tokens, first_col, width):
    columns = lax.broadcasted_iota(jnp.int32, (tokens.shape[0], width), 1)
    token_table = ((tokens - first_col)[:, None] == columns).astype(jnp.float32)
    return jnp.dot(
        weights, token_table, precision=lax.Precision.HIGHEST, preferred_element_type=jnp.float32
    )


def body(hidden, lm_head, store_keys, values, licences, allowed):
    own_cols = lm_head.shape[1]
    inverse_root = 1.0 / math.sqrt(store_keys.shape[1])
    wide_keys = store_keys.astype(jnp.float32)
    key_half = 0.5 * jnp.sum(wide_keys * wide_keys, axis=1) * inverse_root
    portion = lax.all_gather(hidden, "store", axis=0, tiled=True)
    logit_rows = jnp.dot(portion, lm_head, preferred_element_type=jnp.float32)
    score_rows = lax.dot_general(
        portion, store_keys, (((1,), (1,)), ((), ())), preferred_element_type=jnp.float32
    )
    joined = jnp.concatenate([logit_rows, score_rows * inverse_root - key_half[None, :]], axis=1)
    logits = joined[:, :own_cols]
    scores = joined[:, own_cols:]
    permitted = jnp.bitwise_and(jnp.right_shift(allowed[:, None], licences[None, :]), 1) == 1
    masked = jnp.where(permitted, scores, NEG_FILL)
    lm_max, knn_max = lax.pmax(
        (jnp.max(logits, axis=1), jnp.max(masked, axis=1)), ("store", "vocab")
    )
    lm_terms = jnp.exp(logits - lm_max[:, None])
    kernel = jnp.where(permitted, jnp.exp(masked - knn_max[:, None]), 0.0)
    lm_total, knn_total = lax.psum(
        (jnp.sum(lm_terms, axis=1), jnp.sum(kernel, axis=1)), ("store", "vocab")
    )
    lm_log = logits - lm_max[:, None] - jnp.log(lm_total)[:, None]
    received, sources = (
        lax.all_to_all(
            kernel.astype(jnp.bfloat16), "vocab", split_axis=1, concat_axis=1, tiled=True
        ).astype(kernel.dtype),
        lax.all_to_all(values[None, :], "vocab", split_axis=1, concat_axis=1, tiled=True),
    )
    first_col = (
        lax.axis_index("store") * lax.axis_size("vocab") + lax.axis_index("vocab")
    ) * own_cols
    knn_mass = bin_tokens(received, sources[0], first_col, own_cols)
    return mixture(lm_log, knn_mass, knn_total)


def solution(mesh):
    return jax.shard_map(
        body,
        mesh=mesh,
        in_specs=(
            P("store", None),
            P(None, ("store", "vocab")),
            P(("store", "vocab"), None),
            P(("store", "vocab")),
            P(("store", "vocab")),
            P(),
        ),
        out_specs=P(None, ("store", "vocab")),
        check_vma=False,
    )
```

profile of v0, /device:TPU:0, one launch (start us, length us, event | category | flops | bytes accessed | tf_op | source)
XLA Modules:
  0.0 170.6 jit_solution(7530144514574135348)
XLA Ops:
  6.5 0.0 all-gather.2.cloned.1.call-start
  6.5 0.7 all-gather.2.cloned.1.call-update
  7.3 1.3 all_to_all.17
  8.6 6.3 %all-to-all-start.1 = ((s32[1,4,64]{2,0,1:T(1,128)}), s32[1,4,64]{2,0,1:T(1,128)S(1)}, u32[]{:S(2)}, u32[]{:S(2)}) async-start(s32[1,4,64]{2,0,1:T(1,128)} %all_to_all.17), calls=%async_computation.1 | async-start | bytes 4096 | tf_op jit(solution)/shard_map/all_to_all | solution.py:53
  14.9 2.1 %multiply_reduce_fusion = f32[256]{0:T(256)S(1)} fusion(bf16[256,4096]{1,0:T(8,128)(2,1)} %param.8), kind=kLoop, calls=%fused_computation.5 | loop fusion | flops 3145472 | bytes 2098176 | tf_op jit(solution)/shard_map/reduce_sum | solution.py:29
  17.0 0.0 copy-start
  17.0 0.0 copy-start.1
  17.0 0.0 copy-start.2
  17.0 31.7 %all-gather.2.cloned.1.call-done = bf16[512,4096]{1,0:T(8,128)(2,1)} async-done(((bf16[64,4096]{1,0:T(8,128)(2,1)}), bf16[512,4096]{1,0:T(8,128)(2,1)}) %all-gather.2.cloned.1.call-update) | async-done | bytes 4194320 | tf_op jit(solution)/shard_map/all_gather | solution.py:30
  48.7 0.0 copy-start.3
  48.7 17.1 %fusion.8 = (f32[512]{0:T(512)S(1)}, f32[512,2048]{1,0:T(8,128)}) fusion(bf16[512,4096]{1,0:T(8,128)(2,1)} %all-gather.2.cloned.1.call-done, bf16[4096,2048]{1,0:T(8,128)(2,1)} %param.7), kind=kOutput, calls=%fused_computation.20 | convolution fusion | flops 8590983168 | bytes 25167872 | tf_op jit(solution)/shard_map/dot_general | solution.py:31
  65.8 0.0 copy-done
  65.8 0.0 copy-done.1
  65.8 0.0 copy-done.2
  65.8 0.0 copy-done.3
  65.8 1.3 fusion.7
  67.1 39.4 %all-reduce.1 = (f32[512]{0:T(512)S(1)}, f32[512]{0:T(512)S(1)}) all-reduce(f32[512]{0:T(512)S(1)} %get-tuple-element.11, f32[512]{0:T(512)S(1)} %get-tuple-element.13), channel_id=1, replica_groups=mesh['store'=8,'vocab'=4] {'store','vocab'}, use_global_device_ids=true, to_apply=%region_6.7 | all-reduce | flops 1024 | bytes 8192 | tf_op jit(solution)/shard_map/pmax | solution.py:40
  106.5 0.9 fusion.5
  107.3 0.0 all-to-all-done.1
  107.3 3.6 %all-to-all-start = ((bf16[512,4,64]{0,2,1:T(8,128)(2,1)}), bf16[512,4,64]{0,2,1:T(8,128)(2,1)S(1)}, u32[]{:S(2)}, u32[]{:S(2)}) async-start(bf16[512,4,64]{0,2,1:T(8,128)(2,1)} %bitcast), calls=%async_computation | async-start | bytes 524288 | tf_op jit(solution)/shard_map/all_to_all | solution.py:50
  110.9 0.1 sub.62
  111.0 2.9 %exponential_reduce_fusion = f32[512]{0:T(512)S(1)} fusion(f32[512,2048]{1,0:T(8,128)} %get-tuple-element.14, f32[512]{0:T(512)S(1)} %get-tuple-element.8), kind=kLoop, calls=%fused_computation.7 | loop fusion | flops 2096640 | bytes 4198400 | tf_op jit(solution)/shard_map/reduce_sum | solution.py:46
  113.9 41.6 %all-reduce = (f32[512]{0:T(512)S(1)}, f32[512]{0:T(512)S(1)}) all-reduce(f32[512]{0:T(512)S(1)} %get-tuple-element.9, f32[512]{0:T(512)S(1)} %exponential_reduce_fusion), channel_id=1, replica_groups=mesh['store'=8,'vocab'=4] {'store','vocab'}, use_global_device_ids=true, to_apply=%region_8.9 | all-reduce | flops 1024 | bytes 8192 | tf_op jit(solution)/shard_map/psum | solution.py:45
  155.5 0.0 all-to-all-done
  155.5 8.2 %add_select_fusion = f32[512,2048]{1,0:T(8,128)} fusion(f32[512,2048]{1,0:T(8,128)} %get-tuple-element.14, bf16[512,256]{0,1:T(8,128)(2,1)S(1)} %bitcast.7, f32[512]{0:T(512)S(1)} %get-tuple-element.5, f32[512]{0:T(512)S(1)} %log.6, f32[512]{0:T(512)S(1)} %get-tuple-element.8, s32[256]{0:T(256)S(1)} %sub.62), kind=kOutput, calls=%fused_computation.4 | convolution fusion | flops 554172416 | bytes 8657920 | tf_op jit(solution)/shard_map/dot_general | solution.py:20
  (3 shorter events, 0.0 us)
Async XLA Ops:
  6.5 42.2 %all-gather.2.cloned.1.call-start = ((), (), s32[]{:S(2)}) async-start(), calls=%async_computation.2 | async-start | bytes 4718592 | tf_op jit(solution)/shard_map/all_gather | solution.py:30
  8.6 98.7 %all-to-all-start.1 = ((s32[1,4,64]{2,0,1:T(1,128)}), s32[1,4,64]{2,0,1:T(1,128)S(1)}, u32[]{:S(2)}, u32[]{:S(2)}) async-start(s32[1,4,64]{2,0,1:T(1,128)} %all_to_all.17), calls=%async_computation.1 | async-start | bytes 4096 | tf_op jit(solution)/shard_map/all_to_all | solution.py:53
  17.0 48.8 %copy-start = (bf16[256,4096]{1,0:T(8,128)(2,1)S(1)}, bf16[256,4096]{1,0:T(8,128)(2,1)}, u32[]{:S(2)}) copy-start(bf16[256,4096]{1,0:T(8,128)(2,1)} %param.8) | copy-start | bytes 6291460
  17.0 48.7 %copy-start.1 = (s32[512]{0:T(512)S(1)}, s32[512]{0:T(512)}, u32[]{:S(2)}) copy-start(s32[512]{0:T(512)} %param.11) | copy-start | bytes 6148
  17.0 48.7 %copy-start.2 = (s32[256]{0:T(256)S(1)}, s32[256]{0:T(256)}, u32[]{:S(2)}) copy-start(s32[256]{0:T(256)} %param.10) | copy-start | bytes 3076
  48.7 17.1 %copy-start.3 = (bf16[512,4096]{1,0:T(8,128)(2,1)S(1)}, bf16[512,4096]{1,0:T(8,128)(2,1)}, u32[]{:S(2)}) copy-start(bf16[512,4096]{1,0:T(8,128)(2,1)} %all-gather.2.cloned.1.call-done) | copy-start | bytes 12582916
  107.3 48.2 %all-to-all-start = ((bf16[512,4,64]{0,2,1:T(8,128)(2,1)}), bf16[512,4,64]{0,2,1:T(8,128)(2,1)S(1)}, u32[]{:S(2)}, u32[]{:S(2)}) async-start(bf16[512,4,64]{0,2,1:T(8,128)(2,1)} %bitcast), calls=%async_computation | async-start | bytes 524288 | tf_op jit(solution)/shard_map/all_to_all | solution.py:50
Sparse Core Ops, SparseCore 0:
  9.2 39.4 all-gather.1
where the time goes:
time: 171 us
  blocking collectives  81 us (47%)
  waiting for transfers between devices  32.4 us (19%)
  matrix products  26.6 us (16%)
  between operations  13.4 us (8%)
  starting transfers between devices  9.87 us (6%)
  other arithmetic  5.86 us (3%)
    psum x1, blocking collectives, body(): lax.psum((jnp.sum(lm_terms, axis=1), jnp.sum(kernel, axis=1)), ('store',...  41.6 us
    pmax x1, blocking collectives, body(): lax.pmax((jnp.max(logits, axis=1), jnp.max(masked, axis=1)), ('store', 'v...  39.4 us
    all_gather x1, waiting for transfers between devices, body(): portion = lax.all_gather(hidden, 'store', axis=0, tiled=True)  31.7 us
    dot_general x1, matrix products, body(): logit_rows = jnp.dot(portion, lm_head, preferred_element_type=jnp.float32)  17.1 us
    dot_general x1, matrix products, bin_tokens(): jnp.dot(weights, token_table, precision=lax.Precision.HIGHEST, preferred_...  8.19 us
    all_to_all x1, starting transfers between devices, body(): lax.all_to_all(values[None, :], 'vocab', split_axis=1, concat_axis=1, til...  6.32 us
    all_to_all x1, starting transfers between devices, body(): lax.all_to_all(kernel.astype(jnp.bfloat16), 'vocab', split_axis=1, concat...  3.55 us
  transfers between devices with their start and end apart: 3, of which 1 were waited for; matrix products, arithmetic and copies ran while one was open for 14% of the time, Pallas kernels for 0%

commit v1 on v0

--- a/solution.py
+++ b/solution.py
@@ -43,7 +43,7 @@
     lm_terms = jnp.exp(logits - lm_max[:, None])
     kernel = jnp.where(permitted, jnp.exp(masked - knn_max[:, None]), 0.0)
     lm_total, knn_total = lax.psum(
-        (jnp.sum(lm_terms, axis=1), jnp.sum(kernel, axis=1)), ("store", "vocab")
+        lax.psum((jnp.sum(lm_terms, axis=1), jnp.sum(kernel, axis=1)), "vocab"), "store"
     )
     lm_log = logits - lm_max[:, None] - jnp.log(lm_total)[:, None]
     received, sources = (

time: 171 us -> 154 us (0.901)
  blocking collectives: 81 us -> 63.6 us
    psum x1 -> x2, blocking collectives: 41.6 us -> 24.2 us  [the longest x1 12.2 us: body(): lax.psum((jnp.sum(lm_terms, axis=1), jnp.sum(kernel, axis=1)), 'vocab')]
  transfers between devices with their start and end apart: 3 -> 3, of which waited for: 1 -> 1; matrix products, arithmetic and copies ran while one was open for 14% -> 16% of each run, Pallas kernels for 0% -> 0%
where the time goes in v1:
time: 154 us; the launch traced here: 153 us
  blocking collectives  63.6 us (41%)
  waiting for transfers between devices  32.4 us (21%)
  matrix products  26.6 us (17%)
  between operations  13.4 us (9%)
  starting transfers between devices  9.87 us (6%)
  other arithmetic  5.86 us (4%)
    pmax x1, blocking collectives, body(): lax.pmax((jnp.max(logits, axis=1), jnp.max(masked, axis=1)), ('store', 'v...  39.4 us
    all_gather x1, waiting for transfers between devices, body(): portion = lax.all_gather(hidden, 'store', axis=0, tiled=True)  31.7 us
    dot_general x1, matrix products, body(): logit_rows = jnp.dot(portion, lm_head, preferred_element_type=jnp.float32)  17.1 us
    psum x1, blocking collectives, body(): lax.psum((jnp.sum(lm_terms, axis=1), jnp.sum(kernel, axis=1)), 'vocab')  12.2 us
    psum x1, blocking collectives, body(): lax.psum(lax.psum((jnp.sum(lm_terms, axis=1), jnp.sum(kernel, axis=1)), '...  12 us
    dot_general x1, matrix products, bin_tokens(): jnp.dot(weights, token_table, precision=lax.Precision.HIGHEST, preferred_...  8.19 us
    all_to_all x1, starting transfers between devices, body(): lax.all_to_all(values[None, :], 'vocab', split_axis=1, concat_axis=1, til...  6.32 us
    all_to_all x1, starting transfers between devices, body(): lax.all_to_all(kernel.astype(jnp.bfloat16), 'vocab', split_axis=1, concat...  3.55 us
  transfers between devices with their start and end apart: 3, of which 1 were waited for; matrix products, arithmetic and copies ran while one was open for 16% of the time, Pallas kernels for 0%

profile of v1, /device:TPU:0, one launch (start us, length us, event | category | flops | bytes accessed | tf_op | source)
XLA Modules:
  0.0 153.1 jit_solution(2948822493545727218)
XLA Ops:
  6.5 0.0 all-gather.2.cloned.1.call-start
  6.5 0.7 all-gather.2.cloned.1.call-update
  7.3 1.3 all_to_all.17
  8.6 6.3 %all-to-all-start.1 = ((s32[1,4,64]{2,0,1:T(1,128)}), s32[1,4,64]{2,0,1:T(1,128)S(1)}, u32[]{:S(2)}, u32[]{:S(2)}) async-start(s32[1,4,64]{2,0,1:T(1,128)} %all_to_all.17), calls=%async_computation.1 | async-start | bytes 4096 | tf_op jit(solution)/shard_map/all_to_all | solution.py:53
  14.9 2.1 %multiply_reduce_fusion = f32[256]{0:T(256)S(1)} fusion(bf16[256,4096]{1,0:T(8,128)(2,1)} %param.8), kind=kLoop, calls=%fused_computation.5 | loop fusion | flops 3145472 | bytes 2098176 | tf_op jit(solution)/shard_map/reduce_sum | solution.py:29
  17.0 0.0 copy-start
  17.0 0.0 copy-start.1
  17.0 0.0 copy-start.2
  17.0 31.7 %all-gather.2.cloned.1.call-done = bf16[512,4096]{1,0:T(8,128)(2,1)} async-done(((bf16[64,4096]{1,0:T(8,128)(2,1)}), bf16[512,4096]{1,0:T(8,128)(2,1)}) %all-gather.2.cloned.1.call-update) | async-done | bytes 4194320 | tf_op jit(solution)/shard_map/all_gather | solution.py:30
  48.7 0.0 copy-start.3
  48.7 17.1 %fusion.8 = (f32[512]{0:T(512)S(1)}, f32[512,2048]{1,0:T(8,128)}) fusion(bf16[512,4096]{1,0:T(8,128)(2,1)} %all-gather.2.cloned.1.call-done, bf16[4096,2048]{1,0:T(8,128)(2,1)} %param.7), kind=kOutput, calls=%fused_computation.20 | convolution fusion | flops 8590983168 | bytes 25167872 | tf_op jit(solution)/shard_map/dot_general | solution.py:31
  65.8 0.0 copy-done
  65.8 0.0 copy-done.1
  65.8 0.0 copy-done.2
  65.8 0.0 copy-done.3
  65.8 1.3 fusion.7
  67.1 39.4 %all-reduce = (f32[512]{0:T(512)S(1)}, f32[512]{0:T(512)S(1)}) all-reduce(f32[512]{0:T(512)S(1)} %get-tuple-element.13, f32[512]{0:T(512)S(1)} %get-tuple-element.15), channel_id=1, replica_groups=mesh['store'=8,'vocab'=4] {'store','vocab'}, use_global_device_ids=true, to_apply=%region_7.8 | all-reduce | flops 1024 | bytes 8192 | tf_op jit(solution)/shard_map/pmax | solution.py:40
  106.5 0.9 fusion.5
  107.3 0.0 all-to-all-done.1
  107.3 3.6 %all-to-all-start = ((bf16[512,4,64]{0,2,1:T(8,128)(2,1)}), bf16[512,4,64]{0,2,1:T(8,128)(2,1)S(1)}, u32[]{:S(2)}, u32[]{:S(2)}) async-start(bf16[512,4,64]{0,2,1:T(8,128)(2,1)} %bitcast), calls=%async_computation | async-start | bytes 524288 | tf_op jit(solution)/shard_map/all_to_all | solution.py:50
  110.9 0.1 sub.62
  111.0 2.9 %exponential_reduce_fusion = f32[512]{0:T(512)S(1)} fusion(f32[512,2048]{1,0:T(8,128)} %get-tuple-element.16, f32[512]{0:T(512)S(1)} %get-tuple-element.6), kind=kLoop, calls=%fused_computation.7 | loop fusion | flops 2096640 | bytes 4198400 | tf_op jit(solution)/shard_map/reduce_sum | solution.py:46
  113.9 12.2 %all-reduce.2 = (f32[512]{0:T(512)S(1)}, f32[512]{0:T(512)S(1)}) all-reduce(f32[512]{0:T(512)S(1)} %get-tuple-element.11, f32[512]{0:T(512)S(1)} %exponential_reduce_fusion), channel_id=1, replica_groups=mesh['store'=8,'vocab'=4] {'vocab'}, use_global_device_ids=true, to_apply=%region_9.10 | all-reduce | flops 1024 | bytes 8192 | tf_op jit(solution)/shard_map/psum | solution.py:46
  126.1 12.0 %all-reduce.1 = (f32[512]{0:T(512)S(1)}, f32[512]{0:T(512)S(1)}) all-reduce(f32[512]{0:T(512)S(1)} %get-tuple-element.9, f32[512]{0:T(512)S(1)} %get-tuple-element.10), channel_id=1, replica_groups=mesh['store'=8,'vocab'=4] {'store'}, use_global_device_ids=true, to_apply=%region_10.11 | all-reduce | flops 1024 | bytes 8192 | tf_op jit(solution)/shard_map/psum | solution.py:45
  138.1 0.0 all-to-all-done
  138.1 8.2 %add_select_fusion = f32[512,2048]{1,0:T(8,128)} fusion(f32[512,2048]{1,0:T(8,128)} %get-tuple-element.16, bf16[512,256]{0,1:T(8,128)(2,1)S(1)} %bitcast.7, f32[512]{0:T(512)S(1)} %get-tuple-element.7, f32[512]{0:T(512)S(1)} %log.6, f32[512]{0:T(512)S(1)} %get-tuple-element.6, s32[256]{0:T(256)S(1)} %sub.62), kind=kOutput, calls=%fused_computation.4 | convolution fusion | flops 554172416 | bytes 8657920 | tf_op jit(solution)/shard_map/dot_general | solution.py:20
  (3 shorter events, 0.0 us)
Async XLA Ops:
  6.5 42.2 %all-gather.2.cloned.1.call-start = ((), (), s32[]{:S(2)}) async-start(), calls=%async_computation.2 | async-start | bytes 4718592 | tf_op jit(solution)/shard_map/all_gather | solution.py:30
  8.6 98.7 %all-to-all-start.1 = ((s32[1,4,64]{2,0,1:T(1,128)}), s32[1,4,64]{2,0,1:T(1,128)S(1)}, u32[]{:S(2)}, u32[]{:S(2)}) async-start(s32[1,4,64]{2,0,1:T(1,128)} %all_to_all.17), calls=%async_computation.1 | async-start | bytes 4096 | tf_op jit(solution)/shard_map/all_to_all | solution.py:53
  17.0 48.8 %copy-start = (bf16[256,4096]{1,0:T(8,128)(2,1)S(1)}, bf16[256,4096]{1,0:T(8,128)(2,1)}, u32[]{:S(2)}) copy-start(bf16[256,4096]{1,0:T(8,128)(2,1)} %param.8) | copy-start | bytes 6291460
  17.0 48.7 %copy-start.1 = (s32[512]{0:T(512)S(1)}, s32[512]{0:T(512)}, u32[]{:S(2)}) copy-start(s32[512]{0:T(512)} %param.11) | copy-start | bytes 6148
  17.0 48.7 %copy-start.2 = (s32[256]{0:T(256)S(1)}, s32[256]{0:T(256)}, u32[]{:S(2)}) copy-start(s32[256]{0:T(256)} %param.10) | copy-start | bytes 3076
  48.7 17.1 %copy-start.3 = (bf16[512,4096]{1,0:T(8,128)(2,1)S(1)}, bf16[512,4096]{1,0:T(8,128)(2,1)}, u32[]{:S(2)}) copy-start(bf16[512,4096]{1,0:T(8,128)(2,1)} %all-gather.2.cloned.1.call-done) | copy-start | bytes 12582916
  107.3 30.8 %all-to-all-start = ((bf16[512,4,64]{0,2,1:T(8,128)(2,1)}), bf16[512,4,64]{0,2,1:T(8,128)(2,1)S(1)}, u32[]{:S(2)}, u32[]{:S(2)}) async-start(bf16[512,4,64]{0,2,1:T(8,128)(2,1)} %bitcast), calls=%async_computation | async-start | bytes 524288 | tf_op jit(solution)/shard_map/all_to_all | solution.py:50
Sparse Core Ops, SparseCore 0:
  9.2 39.4 all-gather.1
